TPU v7x, 32 devices: a whole 2x2x4 slice. The times are simulated.
32 devices in a mesh: row: 8 (over y, x, core), col: 4 (over z).
Axes of the slice: x: 2, y: 2, z: 4, core: 2. Of those that a mesh axis runs over, the one named last changes fastest.
Arguments:
- inverse_rows: float32 [16384, 16384], P('col', 'row'), may hold values from -0.5 to 0.5
- panels: float32 [4, 16384, 256], P('col', 'row'), may hold values from -0.75 to 0.75
- diag_inverse: float32 [2, 256, 256], replicated, may hold values from -12 to 12
- pattern: int32 [2, 64], replicated, may hold values 0 or 1
- owner_slot: int32 [2], replicated, may hold values from 0 to 3, as said below
Outputs:
- inverse_column: float32 [2, 16384, 256], P(None, 'row')
- inverse_row: float32 [2, 256, 16384], P(None, None, 'col')
- diag_block: float32 [2, 256, 256], replicated
Inputs may be any that keep to these rules, and one draw needn't show every extreme that they name: `owner_slot`: the two supernodes' panels lie in two different slots, one of them the last slot.
All inputs are finite; a program needn't handle non-finite values.
Results may differ from a plain program's by a relative error of at most 0.0001.
Values sent between devices are 32-bit elements; how exact they have to be, the bound alone decides.
A program may use at most 128 MiB of HBM per device.

v0:
```python
import jax
import jax.numpy as jnp
from jax import lax
from jax.sharding import PartitionSpec as P


def from_root(array, axis, root):
    mine = lax.axis_index(axis) == root
    return lax.psum(jnp.where(mine, array, jnp.zeros_like(array)), axis)


def block_mask(pattern_row, start_block, count_blocks, width):
    live = lax.dynamic_slice_in_dim(pattern_row, start_block, count_blocks, 0).astype(jnp.float32)
    return jnp.repeat(live, width)


def shards(inverse_rows, panels, diag_inverse, pattern, owner_slot):
    n_rows = lax.axis_size("row")
    n_cols = lax.axis_size("col")
    row_index = lax.axis_index("row")
    col_index = lax.axis_index("col")
    rows_here = panels.shape[1]
    cols_here = inverse_rows.shape[0]
    width = panels.shape[2]
    blocks = pattern.shape[1]
    source_col = row_index * n_cols // n_rows
    start_row = row_index * rows_here - source_col * cols_here
    masked_list = []
    colmask_list = []
    for number in range(2):
        mask_rows = block_mask(
            pattern[number], row_index * (blocks // n_rows), blocks // n_rows, width
        )
        mask_cols = block_mask(
            pattern[number], col_index * (blocks // n_cols), blocks // n_cols, width
        )
        held = from_root(panels[0], "col", owner_slot[number])
        masked_list.append(mask_rows[:, None] * held)
        colmask_list.append(mask_cols)
    masked_all = jnp.stack(masked_list)
    colmask_all = jnp.stack(colmask_list)
    partial_value = jnp.einsum(
        "ij,sjw->siw", inverse_rows, masked_all, precision=lax.Precision.HIGHEST
    )
    column_total = lax.psum(partial_value, "row")
    column = -(colmask_all[:, :, None] * column_total)
    piece = lax.dynamic_slice_in_dim(column, start_row, rows_here, 1)
    lower = from_root(piece, "col", source_col)
    inner = jnp.einsum("sjw,sjv->swv", masked_all, lower, precision=lax.Precision.HIGHEST)
    diagonal = diag_inverse - lax.psum(inner, "row")
    return (lower, jnp.swapaxes(column, 1, 2), diagonal)


def solution(mesh):
    in_specs = (P("col", "row"), P("col", "row", None), P(), P(), P())
    out_specs = (P(None, "row", None), P(None, None, "col"), P())
    return jax.shard_map(shards, mesh=mesh, in_specs=in_specs, out_specs=out_specs, check_vma=False)
```

profile of v0, /device:TPU:0, one launch (start us, length us, event | category | flops | bytes accessed | tf_op | source)
XLA Modules:
  0.0 592.8 jit_solution(14428068676685210212)
XLA Ops:
  7.2 0.0 all-reduce.12.cloned.1.call-start
  7.2 1.3 fusion.17
  9.8 1.9 copy.8
  11.8 0.0 copy-start.2
  11.8 2.5 select_bitcast_fusion.1
  14.3 0.0 all-reduce.12.cloned.1.call-update
  14.3 0.0 all-reduce.6.cloned.1.call-start
  14.4 0.0 copy-done.2
  14.4 0.1 fusion.11
  14.5 0.1 broadcast_bitcast_fusion.3
  14.6 0.1 fusion.13
  14.6 0.1 broadcast_bitcast_fusion.2
  14.7 157.5 %all-reduce.12.cloned.1.call-done = (f32[2048,256]{0,1:T(8,128)}, f32[2048,256]{0,1:T(8,128)}) async-done(((f32[2048,256]{0,1:T(8,128)}, f32[2048,256]{0,1:T(8,128)}), (f32[2048,256]{0,1:T(8,128)}, f32[2048,256]{0,1:T(8,128)})) %all-reduce.12.cloned.1.call-update) | async-done | bytes 4194320 | tf_op jit(solution)/shard_map/psum | solution.py:9
  172.2 2.6 multiply_bitcast_fusion
  174.8 0.0 copy-start
  174.8 1.3 copy-done
  176.1 59.4 %fusion.2 = f32[2,4096,256]{1,2,0:T(8,128)} fusion(f32[4096,2048]{1,0:T(8,128)} %param.5, f32[1,2048,256]{1,2,0:T(8,128)S(1)} %get-tuple-element.14, f32[1,2048,256]{1,2,0:T(8,128)S(1)} %get-tuple-element.15), kind=kOutput, calls=%fused_computation.3 | convolution fusion | flops 51540656128 | bytes 46137344 | tf_op jit(solution)/shard_map/ij,sjw->siw/dot_general | solution.py:42
  235.5 0.0 all-reduce.6.cloned.1.call-update
  235.5 0.0 all-reduce.8.cloned.1.call-start
  235.6 0.1 fusion.7
  235.7 0.1 broadcast_bitcast_fusion.1
  235.8 0.1 broadcast_bitcast_fusion
  235.9 125.0 %all-reduce.6.cloned.1.call-done = f32[2,4096,256]{1,2,0:T(8,128)} async-done(((f32[2,4096,256]{1,2,0:T(8,128)}), f32[2,4096,256]{1,2,0:T(8,128)}) %all-reduce.6.cloned.1.call-update) | async-done | bytes 8388624 | tf_op jit(solution)/shard_map/psum | solution.py:45
  360.9 4.3 multiply_negate_fusion
  365.2 2.3 dynamic-slice_select_fusion
  367.5 0.0 all-reduce.8.cloned.1.call-update
  367.5 0.0 all-reduce.10.cloned.1.call-start
  367.6 155.2 %all-reduce.8.cloned.1.call-done = f32[2,2048,256]{1,2,0:T(8,128)} async-done(((f32[2,2048,256]{1,2,0:T(8,128)}), f32[2,2048,256]{1,2,0:T(8,128)}) %all-reduce.8.cloned.1.call-update) | async-done | bytes 4194320 | tf_op jit(solution)/shard_map/psum | solution.py:9
  522.8 7.6 %fusion.5 = f32[2,256,256]{2,1,0:T(8,128)} fusion(f32[2,2048,256]{1,2,0:T(8,128)} %all-reduce.8.cloned.1.call-done, f32[1,2048,256]{1,2,0:T(8,128)S(1)} %get-tuple-element.14, f32[1,2048,256]{1,2,0:T(8,128)} %copy-done), kind=kOutput, calls=%fused_computation.6 | convolution fusion | flops 3222274048 | bytes 8912896 | tf_op jit(solution)/shard_map/sjw,sjv->swv/dot_general | solution.py:49
  530.4 0.0 all-reduce.10.cloned.1.call-update
  530.4 8.3 %fusion.19 = f32[2,256,4096]{2,1,0:T(8,128)} fusion(f32[2,4096,256]{1,2,0:T(8,128)} %all-reduce.6.cloned.1.call-done, f32[2,4096]{1,0:T(2,128)S(1)} %pad_maximum_fusion.3), kind=kLoop, calls=%fused_computation.32 | loop fusion | flops 4194304 | bytes 16809984 | tf_op jit(solution)/shard_map/transpose | solution.py:51
  538.7 0.0 copy-start.1
  538.7 5.4 copy.11
  544.1 40.2 %all-reduce.10.cloned.1.call-done = f32[2,256,256]{2,1,0:T(8,128)} async-done(((f32[2,256,256]{2,1,0:T(8,128)}), f32[2,256,256]{2,1,0:T(8,128)}) %all-reduce.10.cloned.1.call-update) | async-done | bytes 524304 | tf_op jit(solution)/shard_map/psum | solution.py:50
  584.3 0.0 copy-done.1
  584.3 1.9 sub.12
  (6 shorter events, 0.1 us)
Async XLA Ops:
  7.2 165.1 %all-reduce.12.cloned.1.call-start = ((), (), s32[]{:S(2)}) async-start(), calls=%async_computation.3 | async-start | bytes 8388608 | tf_op jit(solution)/shard_map/psum | solution.py:9
  11.8 2.6 copy-start.2
  14.3 346.6 %all-reduce.6.cloned.1.call-start = ((), (), s32[]{:S(2)}) async-start(), calls=%async_computation | async-start | bytes 16777216 | tf_op jit(solution)/shard_map/psum | solution.py:45
  174.8 1.3 copy-start
  235.5 287.3 %all-reduce.8.cloned.1.call-start = ((), (), s32[]{:S(2)}) async-start(), calls=%async_computation.1 | async-start | bytes 8388608 | tf_op jit(solution)/shard_map/psum | solution.py:9
  367.5 216.8 %all-reduce.10.cloned.1.call-start = ((), (), s32[]{:S(2)}) async-start(), calls=%async_computation.2 | async-start | bytes 1048576 | tf_op jit(solution)/shard_map/psum | solution.py:50
  538.7 45.6 %copy-start.1 = (f32[2,256,256]{2,1,0:T(8,128)S(1)}, f32[2,256,256]{2,1,0:T(8,128)}, u32[]{:S(2)}) copy-start(f32[2,256,256]{2,1,0:T(8,128)} %param.7) | copy-start | bytes 1572868
Sparse Core Ops, SparseCore 0:
  14.4 157.7 all-reduce.11
  235.7 125.1 all-reduce.5
  367.7 155.1 all-reduce.7
  530.5 53.7 all-reduce.9
where the time goes:
time: 593 us
  waiting for transfers between devices  478 us (81%)
  matrix products  67 us (11%)
  other arithmetic  22.1 us (4%)
  between operations  15.2 us (3%)
  local copies, waits for them, and re-layouts  10.3 us (2%)
    psum x2, waiting for transfers between devices, from_root(): return lax.psum(jnp.where(mine, array, jnp.zeros_like(array)), axis)  313 us
    psum x1, waiting for transfers between devices, shards(): column_total = lax.psum(partial_value, 'row')  125 us
    dot_general x1, matrix products, shards(): jnp.einsum('ij,sjw->siw', inverse_rows, masked_all, precision=lax.Precisi...  59.4 us
    psum x1, waiting for transfers between devices, shards(): diagonal = diag_inverse - lax.psum(inner, 'row')  40.2 us
  transfers between devices with their start and end apart: 4, of which 4 were waited for; matrix products, arithmetic and copies ran while one was open for 2% of the time, Pallas kernels for 0%

commit v1 on v0

--- a/solution.py
+++ b/solution.py
@@ -42,7 +42,11 @@
     partial_value = jnp.einsum(
         "ij,sjw->siw", inverse_rows, masked_all, precision=lax.Precision.HIGHEST
     )
-    column_total = lax.psum(partial_value, "row")
+    column_total = partial_value
+    for hop in (1, 2, 4):
+        column_total = column_total + lax.ppermute(
+            column_total, "row", [(dev, dev ^ hop) for dev in range(8)]
+        )
     column = -(colmask_all[:, :, None] * column_total)
     piece = lax.dynamic_slice_in_dim(column, start_row, rows_here, 1)
     lower = from_root(piece, "col", source_col)

time: 593 us -> 879 us (1.48)
  waiting for transfers between devices: 478 us -> 735 us
  other arithmetic: 22.1 us -> 46.4 us
    ppermute x0 -> x3, waiting for transfers between devices: none -> 375 us  [shards(): lax.ppermute(column_total, 'row', [(dev, dev ^ hop) for dev in range(8)])]
    psum x1 -> x0, waiting for transfers between devices: 125 us -> none  [shards(): column_total = lax.psum(partial_value, 'row')]
    add x0 -> x2, other arithmetic: none -> 22.6 us  [shards(): column_total + lax.ppermute(column_total, 'row', [(dev, dev ^ hop) for de...]
  transfers between devices with their start and end apart: 4 -> 6, of which waited for: 4 -> 6; matrix products, arithmetic and copies ran while one was open for 2% -> 1% of each run, Pallas kernels for 0% -> 0%
where the time goes in v1:
time: 879 us
  waiting for transfers between devices  735 us (84%)
  matrix products  66.6 us (8%)
  other arithmetic  46.4 us (5%)
  between operations  15.2 us (2%)
  local copies, waits for them, and re-layouts  12.4 us (1%)
    ppermute x3, waiting for transfers between devices, shards(): lax.ppermute(column_total, 'row', [(dev, dev ^ hop) for dev in range(8)])  375 us
    psum x2, waiting for transfers between devices, from_root(): return lax.psum(jnp.where(mine, array, jnp.zeros_like(array)), axis)  312 us
    dot_general x1, matrix products, shards(): jnp.einsum('ij,sjw->siw', inverse_rows, masked_all, precision=lax.Precisi...  59.1 us
    psum x1, waiting for transfers between devices, shards(): diagonal = diag_inverse - lax.psum(inner, 'row')  48.5 us
    add x2, other arithmetic, shards(): column_total + lax.ppermute(column_total, 'row', [(dev, dev ^ hop) for de...  22.6 us
  transfers between devices with their start and end apart: 6, of which 6 were waited for; matrix products, arithmetic and copies ran while one was open for 1% of the time, Pallas kernels for 0%

profile of v1, /device:TPU:0, one launch (start us, length us, event | category | flops | bytes accessed | tf_op | source)
XLA Modules:
  0.0 878.7 jit_solution(15181842736916401670)
XLA Ops:
  7.2 0.0 all-reduce.9.cloned.1.call-start
  7.2 1.3 fusion.17
  9.8 1.9 copy.8
  11.8 0.0 copy-start.3
  11.8 2.5 select_bitcast_fusion.1
  14.3 0.0 all-reduce.9.cloned.1.call-update
  14.3 0.0 all-reduce.5.cloned.1.call-start
  14.4 0.0 copy-done.3
  14.4 0.1 fusion.13
  14.5 0.1 broadcast_bitcast_fusion.2
  14.6 0.1 fusion.11
  14.6 0.1 broadcast_bitcast_fusion.3
  14.7 157.5 %all-reduce.9.cloned.1.call-done = (f32[2048,256]{0,1:T(8,128)}, f32[2048,256]{0,1:T(8,128)}) async-done(((f32[2048,256]{0,1:T(8,128)}, f32[2048,256]{0,1:T(8,128)}), (f32[2048,256]{0,1:T(8,128)}, f32[2048,256]{0,1:T(8,128)})) %all-reduce.9.cloned.1.call-update) | async-done | bytes 4194320 | tf_op jit(solution)/shard_map/psum | solution.py:9
  172.2 2.6 multiply_bitcast_fusion
  174.8 0.0 copy-start.1
  174.8 59.1 %fusion.2 = f32[2,4096,256]{1,2,0:T(8,128)S(1)} fusion(f32[4096,2048]{1,0:T(8,128)} %param.5, f32[1,2048,256]{1,2,0:T(8,128)S(1)} %get-tuple-element.14, f32[1,2048,256]{1,2,0:T(8,128)S(1)} %get-tuple-element.15), kind=kOutput, calls=%fused_computation.3 | convolution fusion | flops 51540656128 | bytes 46137344 | tf_op jit(solution)/shard_map/ij,sjw->siw/dot_general | solution.py:42
  233.9 0.0 copy-done.1
  233.9 0.0 copy-start
  233.9 3.4 copy-done
  237.3 0.0 collective-permute-start
  237.3 13.3 %collective-permute-done = f32[2,4096,256]{1,2,0:T(8,128)} collective-permute-done((f32[2,4096,256]{1,2,0:T(8,128)S(1)}, f32[2,4096,256]{1,2,0:T(8,128)}, u32[]{:S(2)}, u32[]{:S(2)}) %collective-permute-start) | collective-permute-done | bytes 8388640 | tf_op jit(solution)/shard_map/ppermute | solution.py:47
  250.6 11.3 %add.31 = f32[2,4096,256]{1,2,0:T(8,128)} add(f32[2,4096,256]{1,2,0:T(8,128)} %copy-done, f32[2,4096,256]{1,2,0:T(8,128)} %collective-permute-done) | non-fusion elementwise | flops 2097152 | bytes 25165824 | tf_op jit(solution)/shard_map/add | solution.py:47
  261.9 1.5 collective-permute-start.1
  263.4 181.3 %collective-permute-done.1 = f32[2,4096,256]{1,2,0:T(8,128)} collective-permute-done((f32[2,4096,256]{1,2,0:T(8,128)}, f32[2,4096,256]{1,2,0:T(8,128)}, u32[]{:S(2)}, u32[]{:S(2)}) %collective-permute-start.1) | collective-permute-done | bytes 8388640 | tf_op jit(solution)/shard_map/ppermute | solution.py:47
  444.7 11.3 %add.32 = f32[2,4096,256]{1,2,0:T(8,128)} add(f32[2,4096,256]{1,2,0:T(8,128)} %add.31, f32[2,4096,256]{1,2,0:T(8,128)} %collective-permute-done.1) | non-fusion elementwise | flops 2097152 | bytes 25165824 | tf_op jit(solution)/shard_map/add | solution.py:47
  456.0 1.5 collective-permute-start.2
  457.5 0.1 fusion.7
  457.6 0.1 broadcast_bitcast_fusion.1
  457.7 0.1 broadcast_bitcast_fusion
  457.8 180.2 %collective-permute-done.2 = f32[2,4096,256]{1,2,0:T(8,128)} collective-permute-done((f32[2,4096,256]{1,2,0:T(8,128)}, f32[2,4096,256]{1,2,0:T(8,128)}, u32[]{:S(2)}, u32[]{:S(2)}) %collective-permute-start.2) | collective-permute-done | bytes 8388640 | tf_op jit(solution)/shard_map/ppermute | solution.py:47
  638.0 11.8 %multiply_negate_fusion = f32[2,4096,256]{1,2,0:T(8,128)} fusion(f32[2,4096,256]{1,2,0:T(8,128)} %add.32, f32[2,4096,256]{1,2,0:T(8,128)} %collective-permute-done.2, f32[2,4096]{1,0:T(2,128)S(1)} %pad_maximum_fusion.3), kind=kLoop, calls=%fused_computation.2 | loop fusion | flops 6291456 | bytes 25198592 | tf_op jit(solution)/shard_map/neg | solution.py:50
  649.8 4.7 dynamic-slice_select_fusion
  654.5 0.0 all-reduce.5.cloned.1.call-update
  654.6 0.0 all-reduce.7.cloned.1.call-start
  654.6 154.1 %all-reduce.5.cloned.1.call-done = f32[2,2048,256]{1,2,0:T(8,128)} async-done(((f32[2,2048,256]{1,2,0:T(8,128)}), f32[2,2048,256]{1,2,0:T(8,128)}) %all-reduce.5.cloned.1.call-update) | async-done | bytes 4194320 | tf_op jit(solution)/shard_map/psum | solution.py:9
  808.7 7.6 fusion.5
  816.3 0.0 all-reduce.7.cloned.1.call-update
  816.3 0.0 copy-start.2
  816.3 5.4 copy.11
  821.7 48.5 %all-reduce.7.cloned.1.call-done = f32[2,256,256]{2,1,0:T(8,128)} async-done(((f32[2,256,256]{2,1,0:T(8,128)}), f32[2,256,256]{2,1,0:T(8,128)}) %all-reduce.7.cloned.1.call-update) | async-done | bytes 524304 | tf_op jit(solution)/shard_map/psum | solution.py:54
  870.2 0.0 copy-done.2
  870.2 1.9 sub.12
  (6 shorter events, 0.1 us)
Async XLA Ops:
  7.2 165.1 %all-reduce.9.cloned.1.call-start = ((), (), s32[]{:S(2)}) async-start(), calls=%async_computation.2 | async-start | bytes 8388608 | tf_op jit(solution)/shard_map/psum | solution.py:9
  11.8 2.6 copy-start.3
  14.3 794.4 %all-reduce.5.cloned.1.call-start = ((), (), s32[]{:S(2)}) async-start(), calls=%async_computation | async-start | bytes 8388608 | tf_op jit(solution)/shard_map/psum | solution.py:9
  174.8 59.1 %copy-start.1 = (f32[1,2048,256]{1,2,0:T(8,128)}, f32[1,2048,256]{1,2,0:T(8,128)S(1)}, u32[]{:S(2)}) copy-start(f32[1,2048,256]{1,2,0:T(8,128)S(1)} %get-tuple-element.15) | copy-start | bytes 6291460
  233.9 3.4 copy-start
  237.3 13.3 %collective-permute-start = (f32[2,4096,256]{1,2,0:T(8,128)S(1)}, f32[2,4096,256]{1,2,0:T(8,128)}, u32[]{:S(2)}, u32[]{:S(2)}) collective-permute-start(f32[2,4096,256]{1,2,0:T(8,128)S(1)} %fusion.2), channel_id=1, source_target_pairs={{0,4},{4,0},{8,12},{12,8},{16,20},{20,16},{24,28},{28,24},{1,5},{5... | collective-permute-start | bytes 25165832 | tf_op jit(solution)/shard_map/ppermute | solution.py:47
  261.9 182.8 %collective-permute-start.1 = (f32[2,4096,256]{1,2,0:T(8,128)}, f32[2,4096,256]{1,2,0:T(8,128)}, u32[]{:S(2)}, u32[]{:S(2)}) collective-permute-start(f32[2,4096,256]{1,2,0:T(8,128)} %add.31), channel_id=1, source_target_pairs={{0,8},{4,12},{8,0},{12,4},{16,24},{20,28},{24,16},{28,20},{1,9},{5... | collective-permute-start | bytes 25165832 | tf_op jit(solution)/shard_map/ppermute | solution.py:47
  456.0 182.0 %collective-permute-start.2 = (f32[2,4096,256]{1,2,0:T(8,128)}, f32[2,4096,256]{1,2,0:T(8,128)}, u32[]{:S(2)}, u32[]{:S(2)}) collective-permute-start(f32[2,4096,256]{1,2,0:T(8,128)} %add.32), channel_id=1, source_target_pairs={{0,16},{4,20},{8,24},{12,28},{16,0},{20,4},{24,8},{28,12},{1,17},{... | collective-permute-start | bytes 25165832 | tf_op jit(solution)/shard_map/ppermute | solution.py:47
  654.6 215.6 %all-reduce.7.cloned.1.call-start = ((), (), s32[]{:S(2)}) async-start(), calls=%async_computation.1 | async-start | bytes 1048576 | tf_op jit(solution)/shard_map/psum | solution.py:54
  816.3 53.9 %copy-start.2 = (f32[2,256,256]{2,1,0:T(8,128)S(1)}, f32[2,256,256]{2,1,0:T(8,128)}, u32[]{:S(2)}) copy-start(f32[2,256,256]{2,1,0:T(8,128)} %param.7) | copy-start | bytes 1572868
Sparse Core Ops, SparseCore 0:
  14.4 157.7 all-reduce.8
  654.7 153.9 all-reduce.4
  816.4 53.7 all-reduce.6
